TPU v7x, 32 devices: a whole 2x2x4 slice. The times are simulated.
32 devices in a mesh: grp: 2 (over y), sv: 4 (over z), tv: 4 (over x, core).
Axes of the slice: x: 2, y: 2, z: 4, core: 2. Of those that a mesh axis runs over, the one named last changes fastest.
Arguments:
- student_states: bfloat16 [512, 1792], P('grp', 'tv'), parts along dimension 0, may hold values from -60 to 60
- teacher_states: bfloat16 [512, 2304], P('grp', 'tv'), parts along dimension 0, may hold values from -60 to 60
- student_queries: bfloat16 [512, 256], P('grp', 'tv'), parts along dimension 0, may hold values from -60 to 60
- teacher_keys: bfloat16 [512, 256], P('grp', 'tv'), parts along dimension 0, may hold values from -6 to 6
- student_targets: int32 [512], P('grp'), parts along dimension 0, may hold values from 0 to 8191
- teacher_targets: int32 [512], P('grp'), parts along dimension 0, may hold values from 0 to 8191
- student_lengths: int32 [4], P('grp'), parts along dimension 0, may hold values from 64 to 128
- teacher_lengths: int32 [4], P('grp'), parts along dimension 0, may hold values from 64 to 128
- to_teacher: bfloat16 [1792, 2304], P('tv', 'sv'), may hold values from -0.125 to 0.125
- to_student: bfloat16 [2304, 1792], P('tv', 'sv'), may hold values from -0.125 to 0.125
- student_head: bfloat16 [1792, 8192], P(None, ('sv', 'tv')), may hold values from -0.125 to 0.125
- teacher_head: bfloat16 [2304, 8192], P(None, ('sv', 'tv')), may hold values from -0.125 to 0.125
Outputs:
- student_loss: float32 [512], P('grp'), parts along dimension 0
- teacher_loss: float32 [512], P('grp'), parts along dimension 0
- student_grad: bfloat16 [512, 8192], P('grp', ('sv', 'tv')), parts along dimension 0
- teacher_grad: bfloat16 [512, 8192], P('grp', ('sv', 'tv')), parts along dimension 0
There are 2 independent parts, one for each index of `grp`. A program takes and returns all parts, laid end to end along the dimension named above; an argument that names none is the same for every part. Nothing has to cross between parts.
All inputs are finite; a program needn't handle non-finite values.
Results may differ from a plain program's by a relative error of at most 0.0086.
Values may be sent and summed in bfloat16 or wider, within the bound.
No kernel may reach another device: no remote copies, remote signals or barrier semaphores. Data moves between devices by JAX's collectives and lax.ppermute only.
A program may use at most 64 MiB of HBM per device.

v0:
```python
import jax
import jax.numpy as jnp
from jax import lax
from jax.sharding import PartitionSpec as P

DK = 256
floor_value = -1e30


def combined_all(part, axis, combine):
    gathered = jax.tree.map(lambda a: lax.all_gather(a, axis), part)

    def take(source):
        return jax.tree.map(lambda a: lax.dynamic_index_in_dim(a, source, 0, False), gathered)

    return lax.fori_loop(
        1, lax.axis_size(axis), lambda source, state: combine(state, take(source)), take(0)
    )


def align_block(student_queries, teacher_keys, teacher_states, teacher_lengths):
    sequences = teacher_lengths.shape[0]
    query_cols = student_queries.shape[1]
    queries = student_queries.reshape(sequences, -1, query_cols)
    keyset = teacher_keys.reshape(sequences, -1, query_cols)
    partial_scores = jnp.einsum("sid,sjd->sij", queries, keyset, preferred_element_type=jnp.float32)
    scores = lax.psum(partial_scores, "tv") * DK ** (-0.5)
    positions = lax.broadcasted_iota(jnp.int32, scores.shape, 2)
    scores = jnp.where(positions < teacher_lengths[:, None, None], scores, floor_value)
    highest = jnp.max(scores, axis=2, keepdims=True)
    weights = jnp.exp(scores - highest)
    weights = (weights / jnp.sum(weights, axis=2, keepdims=True)).astype(jnp.bfloat16)
    states = teacher_states.reshape(sequences, -1, teacher_states.shape[1])
    aligned = jnp.einsum("sij,sjd->sid", weights, states, preferred_element_type=jnp.float32)
    return aligned.astype(jnp.bfloat16).reshape(-1, teacher_states.shape[1])


def live_rows(row_count, lengths, sequence_length):
    indices = lax.broadcasted_iota(jnp.int32, (row_count,), 0)
    sequence = indices // sequence_length
    position = indices % sequence_length
    owners = lax.broadcasted_iota(jnp.int32, (row_count, lengths.shape[0]), 1)
    length_limit = jnp.sum(jnp.where(sequence[:, None] == owners, lengths[None, :], 0), axis=1)
    return (position < length_limit).astype(jnp.float32)


def local_stats(logits, target_cols, kind_index):
    other_kind = 1 - kind_index
    highest = jnp.max(logits, axis=2)
    scaled = jnp.exp(logits - highest[:, :, None])
    totals = jnp.sum(scaled, axis=2)
    spread = jnp.sum(
        scaled[:, kind_index] * (logits[:, kind_index] - logits[:, other_kind]), axis=1
    )
    column = lax.broadcasted_iota(jnp.int32, logits.shape, 2)
    picked = jnp.sum(jnp.where(column == target_cols[:, None, None], logits, 0.0), axis=2)
    return (highest, totals, spread, picked)


def side_combine(former, latter, kind_index):
    highest = jnp.maximum(former[0], latter[0])
    former_scale = jnp.exp(former[0] - highest)
    latter_scale = jnp.exp(latter[0] - highest)
    totals = former[1] * former_scale + latter[1] * latter_scale
    spread = former[2] * former_scale[:, kind_index] + latter[2] * latter_scale[:, kind_index]
    return (highest, totals, spread, former[3] + latter[3])


def student_combine(former, latter):
    return side_combine(former, latter, 1)


def teacher_combine(former, latter):
    return side_combine(former, latter, 0)


def side_terms(logits, statistics, target_cols):
    highest, totals = (statistics[0], statistics[1])
    log_total = highest + jnp.log(totals)
    chances = jnp.exp(logits - log_total[:, :, None])
    column = lax.broadcasted_iota(jnp.int32, chances[:, 0].shape, 1)
    target_hot = (column == target_cols[:, None]).astype(jnp.float32)
    return (log_total, chances, target_hot)


def student_side(logits, statistics, target_cols, live_mask):
    log_total, chances, target_hot = side_terms(logits, statistics, target_cols)
    totals, spread, picked = (statistics[1], statistics[2], statistics[3])
    diverge = spread / totals[:, 1] - log_total[:, 1] + log_total[:, 0]
    row_loss = live_mask * (
        log_total[:, 0] - picked[:, 0] + log_total[:, 1] - picked[:, 1] + diverge
    )
    gradient = live_mask[:, None] * (2.0 * chances[:, 0] - target_hot - chances[:, 1])
    return (row_loss, gradient.astype(jnp.bfloat16))


def teacher_side(logits, statistics, target_cols, live_mask):
    log_total, chances, target_hot = side_terms(logits, statistics, target_cols)
    totals, spread, picked = (statistics[1], statistics[2], statistics[3])
    diverge = spread / totals[:, 0] - log_total[:, 0] + log_total[:, 1]
    row_loss = live_mask * (diverge + log_total[:, 1] - picked[:, 1])
    gradient = live_mask[:, None] * (2.0 * chances[:, 1] - chances[:, 0] - target_hot)
    return (row_loss, gradient.astype(jnp.bfloat16))


def body(
    student_states,
    teacher_states,
    student_queries,
    teacher_keys,
    student_targets,
    teacher_targets,
    student_lengths,
    teacher_lengths,
    to_teacher,
    to_student,
    student_head,
    teacher_head,
):
    row_total = student_states.shape[0]
    sequence_length = row_total // student_lengths.shape[0]
    sv_index = lax.axis_index("sv")
    tv_index = lax.axis_index("tv")
    tv_count = lax.axis_size("tv")
    vocab_block = sv_index * tv_count + tv_index
    aligned_block = align_block(student_queries, teacher_keys, teacher_states, teacher_lengths)
    full_student = lax.all_gather(student_states, "tv", axis=1, tiled=True)
    full_aligned = lax.all_gather(aligned_block, "tv", axis=1, tiled=True)
    teacher_part = lax.psum(
        jnp.dot(student_states, to_teacher, preferred_element_type=jnp.float32), "tv"
    )
    student_part = lax.psum(
        jnp.dot(aligned_block, to_student, preferred_element_type=jnp.float32), "tv"
    )
    into_teacher = lax.all_gather(teacher_part.astype(jnp.bfloat16), "sv", axis=1, tiled=True)
    into_student = lax.all_gather(student_part.astype(jnp.bfloat16), "sv", axis=1, tiled=True)
    student_logits = jnp.stack(
        [
            jnp.dot(full_student, student_head, preferred_element_type=jnp.float32),
            jnp.dot(into_student, student_head, preferred_element_type=jnp.float32),
        ],
        axis=1,
    )
    student_cols = student_targets - vocab_block * student_head.shape[1]
    student_stats = local_stats(student_logits, student_cols, 1)
    teacher_logits = jnp.stack(
        [
            jnp.dot(full_aligned, teacher_head, preferred_element_type=jnp.float32),
            jnp.dot(into_teacher, teacher_head, preferred_element_type=jnp.float32),
        ],
        axis=1,
    )
    teacher_cols = teacher_targets - vocab_block * teacher_head.shape[1]
    teacher_stats = local_stats(teacher_logits, teacher_cols, 0)
    student_stats = combined_all(student_stats, ("sv", "tv"), student_combine)
    teacher_stats = combined_all(teacher_stats, ("sv", "tv"), teacher_combine)
    every_live = live_rows(row_total, student_lengths, sequence_length)
    student_loss, student_grad = student_side(
        student_logits, student_stats, student_cols, every_live
    )
    teacher_loss, teacher_grad = teacher_side(
        teacher_logits, teacher_stats, teacher_cols, every_live
    )
    return (student_loss, teacher_loss, student_grad, teacher_grad)


def solution(mesh):
    in_specs = (
        P("grp", "tv"),
        P("grp", "tv"),
        P("grp", "tv"),
        P("grp", "tv"),
        P("grp"),
        P("grp"),
        P("grp"),
        P("grp"),
        P("tv", "sv"),
        P("tv", "sv"),
        P(None, ("sv", "tv")),
        P(None, ("sv", "tv")),
    )
    out_specs = (P("grp"), P("grp"), P("grp", ("sv", "tv")), P("grp", ("sv", "tv")))
    return jax.shard_map(body, mesh=mesh, in_specs=in_specs, out_specs=out_specs, check_vma=False)
```

profile of v0, /device:TPU:0, one launch (start us, length us, event | category | flops | bytes accessed | tf_op | source)
XLA Modules:
  0.0 294.7 jit_solution(5090712872728876629)
XLA Ops:
  7.3 1.8 fusion.30
  9.2 12.4 %all_gather.60 = bf16[256,1792]{0,1:T(8,128)(2,1)} all-gather(bf16[256,448]{0,1:T(8,128)(2,1)} %param.16), channel_id=1, replica_groups=mesh['grp'=2,'sv'=4,'tv'=4] {'tv'}, dimensions={1}, use_global_device_ids=true | all-gather | bytes 1146880 | tf_op jit(solution)/shard_map/all_gather | solution.py:127
  21.6 1.3 fusion.60
  23.0 22.0 %all-reduce.4.cloned.1.call-done = f32[2,128,128]{2,1,0:T(8,128)} async-done(((f32[2,128,128]{2,1,0:T(8,128)}), f32[2,128,128]{2,1,0:T(8,128)}) %all-reduce.4.cloned.1.call-update) | async-done | bytes 131088 | tf_op jit(solution)/shard_map/psum | solution.py:27
  45.1 1.2 fusion.56
  46.3 2.4 fusion.5
  48.7 1.5 fusion.48
  50.1 26.0 %all-reduce.5 = (bf16[256,448]{0,1:T(8,128)(2,1)}, bf16[256,576]{0,1:T(8,128)(2,1)}) all-reduce(f32[256,448]{0,1:T(8,128)S(1)} %fusion.48, f32[256,576]{0,1:T(8,128)S(1)} %fusion.60), channel_id=1, replica_groups=mesh['grp'=2,'sv'=4,'tv'=4] {'tv'}, use_global_device_ids=true, to_apply=%region_4.5 | all-reduce | flops 262144 | bytes 1572864 | tf_op jit(solution)/shard_map/psum | solution.py:132
  76.8 2.6 fusion.57
  80.2 33.6 %all_gather.61 = bf16[256,1792]{0,1:T(8,128)(2,1)S(1)} all-gather(bf16[256,448]{0,1:T(8,128)(2,1)S(1)} %copy-done.6), channel_id=1, replica_groups=mesh['grp'=2,'sv'=4,'tv'=4] {'sv'}, dimensions={1}, use_global_device_ids=true | all-gather | bytes 1146880 | tf_op jit(solution)/shard_map/all_gather | solution.py:136
  115.3 20.8 %all-gather.8 = f32[16,1,256]{2,1,0:T(1,128)S(1)} all-gather(f32[1,1,256]{2,1,0:T(1,128)S(1)} %bitcast.187), channel_id=4, replica_groups=mesh['grp'=2,'sv'=4,'tv'=4] {'sv','tv'}, dimensions={0}, use_global_device_ids=true | all-gather | bytes 17408 | tf_op jit(solution)/shard_map/all_gather | solution.py:11
  136.1 17.5 %all-gather = f32[4096,2]{0,1:T(2,128)S(1)} all-gather(f32[256,2]{0,1:T(2,128)S(1)} %get-tuple-element.461), channel_id=2, replica_groups=mesh['grp'=2,'sv'=4,'tv'=4] {'sv','tv'}, dimensions={0}, use_global_device_ids=true | all-gather | bytes 34816 | tf_op jit(solution)/shard_map/all_gather | solution.py:11
  153.6 18.9 %all-gather.1 = f32[4096,2]{0,1:T(2,128)S(1)} all-gather(f32[256,2]{0,1:T(2,128)S(1)} %get-tuple-element.510), channel_id=3, replica_groups=mesh['grp'=2,'sv'=4,'tv'=4] {'sv','tv'}, dimensions={0}, use_global_device_ids=true | all-gather | bytes 34816 | tf_op jit(solution)/shard_map/all_gather | solution.py:11
  172.4 17.5 %all-gather.3 = f32[4096,2]{0,1:T(2,128)S(1)} all-gather(f32[256,2]{0,1:T(2,128)S(1)} %get-tuple-element.460), channel_id=5, replica_groups=mesh['grp'=2,'sv'=4,'tv'=4] {'sv','tv'}, dimensions={0}, use_global_device_ids=true | all-gather | bytes 34816 | tf_op jit(solution)/shard_map/all_gather | solution.py:11
  189.9 1.6 while.42
  193.3 2.9 fusion.61
  196.2 9.7 %all-gather.13.cloned.1.call-done = bf16[256,2304]{0,1:T(8,128)(2,1)} async-done(((bf16[256,576]{0,1:T(8,128)(2,1)}), bf16[256,2304]{0,1:T(8,128)(2,1)}) %all-gather.13.cloned.1.call-update) | async-done | bytes 1179664 | tf_op jit(solution)/shard_map/all_gather | solution.py:128
  205.9 2.1 fusion.59
  208.4 20.5 %all-gather.4 = f32[4096,2]{0,1:T(2,128)S(1)} all-gather(f32[256,2]{0,1:T(2,128)S(1)} %get-tuple-element.459), channel_id=6, replica_groups=mesh['grp'=2,'sv'=4,'tv'=4] {'sv','tv'}, dimensions={0}, use_global_device_ids=true | all-gather | bytes 34816 | tf_op jit(solution)/shard_map/all_gather | solution.py:11
  229.4 17.4 %all-gather.9 = f32[16,1,256]{2,1,0:T(1,128)S(1)} all-gather(f32[1,1,256]{2,1,0:T(1,128)S(1)} %bitcast.188), channel_id=8, replica_groups=mesh['grp'=2,'sv'=4,'tv'=4] {'sv','tv'}, dimensions={0}, use_global_device_ids=true | all-gather | bytes 17408 | tf_op jit(solution)/shard_map/all_gather | solution.py:11
  246.8 18.8 %all-gather.5 = f32[4096,2]{0,1:T(2,128)S(1)} all-gather(f32[256,2]{0,1:T(2,128)S(1)} %get-tuple-element.508), channel_id=7, replica_groups=mesh['grp'=2,'sv'=4,'tv'=4] {'sv','tv'}, dimensions={0}, use_global_device_ids=true | all-gather | bytes 34816 | tf_op jit(solution)/shard_map/all_gather | solution.py:11
  265.7 17.5 %all-gather.7 = f32[4096,2]{0,1:T(2,128)S(1)} all-gather(f32[256,2]{0,1:T(2,128)S(1)} %get-tuple-element.458), channel_id=9, replica_groups=mesh['grp'=2,'sv'=4,'tv'=4] {'sv','tv'}, dimensions={0}, use_global_device_ids=true | all-gather | bytes 34816 | tf_op jit(solution)/shard_map/all_gather | solution.py:11
  283.2 1.6 while.43
  284.8 1.5 subtract_exponential_fusion.2
  (228 shorter events, 9.3 us)
Async XLA Ops:
  7.2 186.1 %copy-start = (bf16[2304,512]{1,0:T(8,128)(2,1)S(1)}, bf16[2304,512]{1,0:T(8,128)(2,1)}, u32[]{:S(2)}) copy-start(bf16[2304,512]{1,0:T(8,128)(2,1)} %param.27) | copy-start | bytes 7077892
  7.2 14.4 %copy-start.5 = (bf16[448,576]{1,0:T(8,128)(2,1)S(1)}, bf16[448,576]{1,0:T(8,128)(2,1)}, u32[]{:S(2)}) copy-start(bf16[448,576]{1,0:T(8,128)(2,1)} %param.24) | copy-start | bytes 1548292
  7.2 15.7 %copy-start.15 = (s32[256]{0:T(256)S(1)}, s32[256]{0:T(256)}, u32[]{:S(2)}) copy-start(s32[256]{0:T(256)} %param.21) | copy-start | bytes 3076
  7.2 15.7 %copy-start.16 = (s32[256]{0:T(256)S(1)}, s32[256]{0:T(256)}, u32[]{:S(2)}) copy-start(s32[256]{0:T(256)} %param.20) | copy-start | bytes 3076
  7.2 15.7 %copy-start.17 = (s32[2]{0:T(128)S(1)}, s32[2]{0:T(128)}, u32[]{:S(2)}) copy-start(s32[2]{0:T(128)} %param.22) | copy-start | bytes 28
  7.2 37.9 %copy-start.18 = (s32[2]{0:T(128)S(1)}, s32[2]{0:T(128)}, u32[]{:S(2)}) copy-start(s32[2]{0:T(128)} %param.23) | copy-start | bytes 28
  7.2 37.9 %all-reduce.4.cloned.1.call-start = ((), (), s32[]{:S(2)}) async-start(), calls=%async_computation | async-start | bytes 262144 | tf_op jit(solution)/shard_map/psum | solution.py:27
  9.1 184.2 %all-gather.15.cloned.1.call-start = ((), (), s32[]{:S(2)}) async-start(), calls=%async_computation.2 | async-start | bytes 1474560 | tf_op jit(solution)/shard_map/all_gather | solution.py:135
  23.0 53.2 %copy-start.7 = (s32[256]{0:T(256)}, s32[256]{0:T(256)S(1)}, u32[]{:S(2)}) copy-start(s32[256]{0:T(256)S(1)} %fusion.35) | copy-start | bytes 3076
  76.2 3.2 %copy-start.4 = (bf16[2,72,8,128]{3,2,1,0:T(8,128)(2,1)S(1)}, bf16[2,72,8,128]{3,2,1,0:T(8,128)(2,1)}, u32[]{:S(2)}) copy-start(bf16[2,72,8,128]{3,2,1,0:T(8,128)(2,1)} %fusion.5) | copy-start | bytes 884740
  76.2 129.7 %all-gather.13.cloned.1.call-start = ((), (), s32[]{:S(2)}) async-start(), calls=%async_computation.1 | async-start | bytes 1474560 | tf_op jit(solution)/shard_map/all_gather | solution.py:128
  76.8 3.4 %copy-start.6 = (bf16[256,448]{0,1:T(8,128)(2,1)S(1)}, bf16[256,448]{0,1:T(8,128)(2,1)}, u32[]{:S(2)}) copy-start(bf16[256,448]{0,1:T(8,128)(2,1)} %get-tuple-element.498) | copy-start | bytes 688132
  76.8 37.0 %copy-start.3 = (bf16[1792,512]{1,0:T(8,128)(2,1)S(1)}, bf16[1792,512]{1,0:T(8,128)(2,1)}, u32[]{:S(2)}) copy-start(bf16[1792,512]{1,0:T(8,128)(2,1)} %param.26) | copy-start | bytes 5505028
  205.9 2.1 copy-start.1
  208.0 21.3 %copy-start.2 = (f32[256,512]{1,0:T(8,128)}, f32[256,512]{1,0:T(8,128)S(1)}, u32[]{:S(2)}) copy-start(f32[256,512]{1,0:T(8,128)S(1)} %fusion.59) | copy-start | bytes 1572868
  284.8 1.6 copy-start.9
  286.4 1.2 copy-start.8
  286.4 1.2 copy-start.10
  286.4 1.2 copy-start.11
  286.4 1.2 copy-start.12
  286.4 1.2 copy-start.13
  286.4 1.2 copy-start.14
Sparse Core Ops, SparseCore 0:
  11.0 34.0 all-reduce.3
  76.3 43.0 all-gather.14
  190.0 15.8 all-gather.12
where the time goes:
time: 295 us
  blocking collectives  221 us (75%)
  waiting for transfers between devices  31.8 us (11%)
  matrix products  15.3 us (5%)
  between operations  14.1 us (5%)
  other arithmetic  8 us (3%)
  local copies, waits for them, and re-layouts  3.24 us (1%)
    all_gather x8, blocking collectives, combined_all(): gathered = jax.tree.map(lambda a: lax.all_gather(a, axis), part)  149 us
    all_gather x1, blocking collectives, body(): lax.all_gather(student_part.astype(jnp.bfloat16), 'sv', axis=1, tiled=True)  33.6 us
    psum x1, blocking collectives, body(): lax.psum(jnp.dot(aligned_block, to_student, preferred_element_type=jnp.fl...  26 us
    psum x1, waiting for transfers between devices, align_block(): scores = lax.psum(partial_scores, 'tv') * DK ** (-0.5)  22 us
    all_gather x1, blocking collectives, body(): full_student = lax.all_gather(student_states, 'tv', axis=1, tiled=True)  12.4 us
    all_gather x1, waiting for transfers between devices, body(): full_aligned = lax.all_gather(aligned_block, 'tv', axis=1, tiled=True)  9.69 us
  transfers between devices with their start and end apart: 3, of which 2 were waited for; matrix products, arithmetic and copies ran while one was open for 4% of the time, Pallas kernels for 0%

commit v1 on v0

--- a/solution.py
+++ b/solution.py
@@ -129,8 +129,11 @@
     teacher_part = lax.psum(
         jnp.dot(student_states, to_teacher, preferred_element_type=jnp.float32), "tv"
     )
-    student_part = lax.psum(
-        jnp.dot(aligned_block, to_student, preferred_element_type=jnp.float32), "tv"
+    student_part = jnp.sum(
+        lax.all_gather(
+            jnp.dot(aligned_block, to_student, preferred_element_type=jnp.float32), "tv"
+        ),
+        axis=0,
     )
     into_teacher = lax.all_gather(teacher_part.astype(jnp.bfloat16), "sv", axis=1, tiled=True)
     into_student = lax.all_gather(student_part.astype(jnp.bfloat16), "sv", axis=1, tiled=True)

time: 295 us -> 276 us (0.936)
  blocking collectives: 221 us -> 195 us
    all_gather x1, blocking collectives: 33.6 us -> 19.8 us  [body(): lax.all_gather(student_part.astype(jnp.bfloat16), 'sv', axis=1, tiled=True)]
    psum x1, waiting for transfers between devices: 22 us -> 14.7 us  [align_block(): scores = lax.psum(partial_scores, 'tv') * DK ** (-0.5)]
    all_gather x1, waiting for transfers between devices: 9.69 us -> 16 us  [body(): full_aligned = lax.all_gather(aligned_block, 'tv', axis=1, tiled=True)]
    psum x1, blocking collectives: 26 us -> 19.8 us  [body(): lax.psum(jnp.dot(student_states, to_teacher, preferred_element_type=jnp.f...]
    all_gather x1, blocking collectives: 12.4 us -> 7.89 us  [body(): full_student = lax.all_gather(student_states, 'tv', axis=1, tiled=True)]
    all_gather x0 -> x1, local copies, waits for them, and re-layouts: none -> 2.97 us  [body(): lax.all_gather(jnp.dot(aligned_block, to_student, preferred_element_type=...]
  transfers between devices with their start and end apart: 3 -> 4, of which waited for: 2 -> 3; matrix products, arithmetic and copies ran while one was open for 4% -> 6% of each run, Pallas kernels for 0% -> 0%
where the time goes in v1:
time: 276 us; the launch traced here: 275 us
  blocking collectives  195 us (71%)
  waiting for transfers between devices  31.4 us (11%)
  between operations  16 us (6%)
  matrix products  14.6 us (5%)
  other arithmetic  10.6 us (4%)
  local copies, waits for them, and re-layouts  6.14 us (2%)
    all_gather x8, blocking collectives, combined_all(): gathered = jax.tree.map(lambda a: lax.all_gather(a, axis), part)  148 us
    psum x1, blocking collectives, body(): lax.psum(jnp.dot(student_states, to_teacher, preferred_element_type=jnp.f...  19.8 us
    all_gather x1, blocking collectives, body(): lax.all_gather(student_part.astype(jnp.bfloat16), 'sv', axis=1, tiled=True)  19.8 us
    all_gather x1, waiting for transfers between devices, body(): full_aligned = lax.all_gather(aligned_block, 'tv', axis=1, tiled=True)  16 us
    psum x1, waiting for transfers between devices, align_block(): scores = lax.psum(partial_scores, 'tv') * DK ** (-0.5)  14.7 us
    all_gather x1, blocking collectives, body(): full_student = lax.all_gather(student_states, 'tv', axis=1, tiled=True)  7.89 us
  transfers between devices with their start and end apart: 4, of which 3 were waited for; matrix products, arithmetic and copies ran while one was open for 6% of the time, Pallas kernels for 0%

profile of v1, /device:TPU:0, one launch (start us, length us, event | category | flops | bytes accessed | tf_op | source)
XLA Modules:
  0.0 275.5 jit_solution(11142467365225751039)
XLA Ops:
  8.1 1.8 fusion.30
  9.9 1.6 fusion.60
  11.6 19.8 %all-reduce.4 = bf16[256,576]{0,1:T(8,128)(2,1)} all-reduce(f32[256,576]{0,1:T(8,128)S(1)} %fusion.60), channel_id=1, replica_groups=mesh['grp'=2,'sv'=4,'tv'=4] {'tv'}, use_global_device_ids=true, to_apply=%region_11.12 | all-reduce | flops 147456 | bytes 884736 | tf_op jit(solution)/shard_map/psum | solution.py:129
  31.5 14.7 %all-reduce.3.cloned.1.call-done = f32[2,128,128]{2,1,0:T(8,128)} async-done(((f32[2,128,128]{2,1,0:T(8,128)}), f32[2,128,128]{2,1,0:T(8,128)}) %all-reduce.3.cloned.1.call-update) | async-done | bytes 131088 | tf_op jit(solution)/shard_map/psum | solution.py:27
  47.3 1.7 fusion.5
  50.5 7.9 %all_gather.66 = bf16[256,1792]{0,1:T(8,128)(2,1)S(1)} all-gather(bf16[256,448]{0,1:T(8,128)(2,1)S(1)} %copy-done.3), channel_id=1, replica_groups=mesh['grp'=2,'sv'=4,'tv'=4] {'tv'}, dimensions={1}, use_global_device_ids=true | all-gather | bytes 1146880 | tf_op jit(solution)/shard_map/all_gather | solution.py:127
  58.4 2.2 fusion.57
  62.5 2.1 fusion.61
  64.6 16.0 %all-gather.15.cloned.1.call-done = bf16[256,2304]{0,1:T(8,128)(2,1)} async-done(((bf16[256,576]{0,1:T(8,128)(2,1)}), bf16[256,2304]{0,1:T(8,128)(2,1)}) %all-gather.15.cloned.1.call-update) | async-done | bytes 1179664 | tf_op jit(solution)/shard_map/all_gather | solution.py:128
  80.6 2.1 fusion.59
  83.5 20.4 %all-gather.10 = f32[16,1,256]{2,1,0:T(1,128)S(1)} all-gather(f32[1,1,256]{2,1,0:T(1,128)S(1)} %bitcast.189), channel_id=9, replica_groups=mesh['grp'=2,'sv'=4,'tv'=4] {'sv','tv'}, dimensions={0}, use_global_device_ids=true | all-gather | bytes 17408 | tf_op jit(solution)/shard_map/all_gather | solution.py:11
  103.9 17.5 %all-gather.5 = f32[4096,2]{0,1:T(2,128)S(1)} all-gather(f32[256,2]{0,1:T(2,128)S(1)} %get-tuple-element.459), channel_id=7, replica_groups=mesh['grp'=2,'sv'=4,'tv'=4] {'sv','tv'}, dimensions={0}, use_global_device_ids=true | all-gather | bytes 34816 | tf_op jit(solution)/shard_map/all_gather | solution.py:11
  121.4 18.9 %all-gather.6 = f32[4096,2]{0,1:T(2,128)S(1)} all-gather(f32[256,2]{0,1:T(2,128)S(1)} %get-tuple-element.506), channel_id=8, replica_groups=mesh['grp'=2,'sv'=4,'tv'=4] {'sv','tv'}, dimensions={0}, use_global_device_ids=true | all-gather | bytes 34816 | tf_op jit(solution)/shard_map/all_gather | solution.py:11
  140.3 17.5 %all-gather.8 = f32[4096,2]{0,1:T(2,128)S(1)} all-gather(f32[256,2]{0,1:T(2,128)S(1)} %get-tuple-element.458), channel_id=10, replica_groups=mesh['grp'=2,'sv'=4,'tv'=4] {'sv','tv'}, dimensions={0}, use_global_device_ids=true | all-gather | bytes 34816 | tf_op jit(solution)/shard_map/all_gather | solution.py:11
  161.0 3.0 %reshape.67 = f32[4,256,448]{1,0,2:T(4,128)} reshape(f32[1024,448]{0,1:T(8,128)} %all-gather.19.cloned.1.call-done) | data formatting | bytes 3670016 | tf_op jit(solution)/shard_map/all_gather | solution.py:133
  164.0 2.6 reduce_sum.83
  166.6 19.8 %all_gather.69 = bf16[256,1792]{0,1:T(8,128)(2,1)S(1)} all-gather(bf16[256,448]{0,1:T(8,128)(2,1)S(1)} %reduce_sum.83), channel_id=1, replica_groups=mesh['grp'=2,'sv'=4,'tv'=4] {'sv'}, dimensions={1}, use_global_device_ids=true | all-gather | bytes 1146880 | tf_op jit(solution)/shard_map/all_gather | solution.py:139
  186.4 2.1 fusion.58
  189.4 19.7 %all-gather.9 = f32[16,1,256]{2,1,0:T(1,128)S(1)} all-gather(f32[1,1,256]{2,1,0:T(1,128)S(1)} %bitcast.190), channel_id=5, replica_groups=mesh['grp'=2,'sv'=4,'tv'=4] {'sv','tv'}, dimensions={0}, use_global_device_ids=true | all-gather | bytes 17408 | tf_op jit(solution)/shard_map/all_gather | solution.py:11
  209.1 17.5 %all-gather.1 = f32[4096,2]{0,1:T(2,128)S(1)} all-gather(f32[256,2]{0,1:T(2,128)S(1)} %get-tuple-element.461), channel_id=3, replica_groups=mesh['grp'=2,'sv'=4,'tv'=4] {'sv','tv'}, dimensions={0}, use_global_device_ids=true | all-gather | bytes 34816 | tf_op jit(solution)/shard_map/all_gather | solution.py:11
  226.6 18.9 %all-gather.2 = f32[4096,2]{0,1:T(2,128)S(1)} all-gather(f32[256,2]{0,1:T(2,128)S(1)} %get-tuple-element.508), channel_id=4, replica_groups=mesh['grp'=2,'sv'=4,'tv'=4] {'sv','tv'}, dimensions={0}, use_global_device_ids=true | all-gather | bytes 34816 | tf_op jit(solution)/shard_map/all_gather | solution.py:11
  245.4 17.5 %all-gather.4 = f32[4096,2]{0,1:T(2,128)S(1)} all-gather(f32[256,2]{0,1:T(2,128)S(1)} %get-tuple-element.460), channel_id=6, replica_groups=mesh['grp'=2,'sv'=4,'tv'=4] {'sv','tv'}, dimensions={0}, use_global_device_ids=true | all-gather | bytes 34816 | tf_op jit(solution)/shard_map/all_gather | solution.py:11
  262.9 1.6 while.42
  264.5 1.5 subtract_exponential_fusion.2
  (227 shorter events, 13.2 us)
Async XLA Ops:
  8.0 54.5 %copy-start = (bf16[2304,512]{1,0:T(8,128)(2,1)S(1)}, bf16[2304,512]{1,0:T(8,128)(2,1)}, u32[]{:S(2)}) copy-start(bf16[2304,512]{1,0:T(8,128)(2,1)} %param.27) | copy-start | bytes 7077892
  8.0 38.1 %copy-start.15 = (s32[2]{0:T(128)S(1)}, s32[2]{0:T(128)}, u32[]{:S(2)}) copy-start(s32[2]{0:T(128)} %param.23) | copy-start | bytes 28
  8.0 38.1 %all-reduce.3.cloned.1.call-start = ((), (), s32[]{:S(2)}) async-start(), calls=%async_computation | async-start | bytes 262144 | tf_op jit(solution)/shard_map/psum | solution.py:27
  9.9 52.6 %all-gather.17.cloned.1.call-start = ((), (), s32[]{:S(2)}) async-start(), calls=%async_computation.2 | async-start | bytes 1474560 | tf_op jit(solution)/shard_map/all_gather | solution.py:138
  11.5 38.3 %copy-start.14 = (s32[2]{0:T(128)S(1)}, s32[2]{0:T(128)}, u32[]{:S(2)}) copy-start(s32[2]{0:T(128)} %param.22) | copy-start | bytes 28
  11.5 38.4 %copy-start.12 = (s32[256]{0:T(256)S(1)}, s32[256]{0:T(256)}, u32[]{:S(2)}) copy-start(s32[256]{0:T(256)} %param.20) | copy-start | bytes 3076
  11.5 38.4 %copy-start.13 = (s32[256]{0:T(256)S(1)}, s32[256]{0:T(256)}, u32[]{:S(2)}) copy-start(s32[256]{0:T(256)} %param.21) | copy-start | bytes 3076
  11.6 39.0 %copy-start.3 = (bf16[256,448]{0,1:T(8,128)(2,1)S(1)}, bf16[256,448]{0,1:T(8,128)(2,1)}, u32[]{:S(2)}) copy-start(bf16[256,448]{0,1:T(8,128)(2,1)} %param.16) | copy-start | bytes 688132
  31.4 49.2 %all-gather.15.cloned.1.call-start = ((), (), s32[]{:S(2)}) async-start(), calls=%async_computation.1 | async-start | bytes 1474560 | tf_op jit(solution)/shard_map/all_gather | solution.py:128
  49.8 111.3 %all-gather.19.cloned.1.call-start = ((), (), s32[]{:S(2)}) async-start(), calls=%async_computation.3 | async-start | bytes 2293760 | tf_op jit(solution)/shard_map/all_gather | solution.py:133
  49.9 10.7 %copy-start.5 = (s32[256]{0:T(256)}, s32[256]{0:T(256)S(1)}, u32[]{:S(2)}) copy-start(s32[256]{0:T(256)S(1)} %fusion.35) | copy-start | bytes 3076
  58.4 2.2 copy-start.4
  64.6 18.7 %copy-start.1 = (f32[256,512]{1,0:T(8,128)}, f32[256,512]{1,0:T(8,128)S(1)}, u32[]{:S(2)}) copy-start(f32[256,512]{1,0:T(8,128)S(1)} %fusion.61) | copy-start | bytes 1572868
  82.6 0.8 copy-start.2
  264.5 1.7 copy-start.7
  266.1 1.2 copy-start.6
  266.1 1.2 copy-start.8
  266.1 1.2 copy-start.9
  266.1 1.2 copy-start.10
  266.1 1.2 copy-start.11
Sparse Core Ops, SparseCore 0:
  11.7 34.3 all-reduce.2
Sparse Core Ops, SparseCore 1:
  31.5 31.0 all-gather.16
  64.0 16.5 all-gather.14
  82.1 21.0 all-gather.18
